TPU v7x, 256 devices: a whole 4x4x8 slice. The times are simulated.
256 devices in a mesh: grp: 8 (over y, x_lo), lay: 32 (over x_hi, z, core).
Axes of the slice: x: 4 (x_hi: 2, x_lo: 2; x = x_hi * 2 + x_lo), y: 4, z: 8, core: 2. Of those that a mesh axis runs over, the one named last changes fastest.
Arguments:
- stored_grads: bfloat16 [8192, 32, 1024], P(('grp', 'lay'))
- inverse_fisher: float32 [32, 1024, 1024], P('lay')
- query_grads: bfloat16 [1024, 32, 1024], P('grp', 'lay'), may hold values from -6 to 6
- example_row: int32 [8, 1024], P('grp'), may hold values from 0 to 1023, each once within a row
- query_slot: int32 [1024], replicated, may hold values from 0 to 1023, each once
Outputs:
- scores: float32 [8192, 1024], P(('grp', 'lay'))
All inputs are finite; a program needn't handle non-finite values.
Results may differ from a plain program's by a relative error of at most 0.0029.
Values may be sent and summed in bfloat16 or wider, within the bound.
A program may use at most 64 MiB of HBM per device.

v0:
```python
import math

import jax
import jax.numpy as jnp
from jax import lax
from jax.sharding import Mesh
from jax.sharding import PartitionSpec as P

LAY = ("lay_0", "lay_1", "lay_2")
GRP_LAY = ("grp", "lay_0", "lay_1", "lay_2")


EPS = 1e-06


def sent_to_all(array, axis):
    copies = jnp.broadcast_to(array, (lax.axis_size(axis), *array.shape))
    return lax.all_to_all(copies, axis, split_axis=0, concat_axis=0, tiled=True)


def in_order(pieces, dim):
    pieces = jnp.moveaxis(pieces, 0, dim)
    shape = pieces.shape
    return pieces.reshape(*shape[:dim], shape[dim] * shape[dim + 1], *shape[dim + 2 :])


def gather_directly(array, axis, dim):
    pieces = sent_to_all(array, axis)
    return in_order(pieces, dim)


def cut_along(array, dim, count):
    before, after = (array.shape[:dim], array.shape[dim + 1 :])
    return jnp.moveaxis(array.reshape(*before, count, -1, *after), dim, 0)


def summed_on_arrival(array, axis, dim):
    pieces = cut_along(array, dim, lax.axis_size(axis))
    arrived = lax.all_to_all(pieces, axis, split_axis=0, concat_axis=0, tiled=True)
    return arrived.sum(axis=0)


def sum_in_two_steps(array, axes, dim):
    far, near = axes
    own = summed_on_arrival(cut_along(array, dim, lax.axis_size(far)), near, dim + 1)
    return jnp.sum(lax.all_to_all(own, far, 0, 0, tiled=True), axis=0)


def score_block(normed_rows, asked):
    return lax.dot_general(
        normed_rows, asked, (((1,), (1,)), ((), ())), preferred_element_type=jnp.float32
    )


def body(stored_grads, inverse_fisher, query_grads, example_row, query_slot):
    owned = lax.all_to_all(stored_grads, LAY, split_axis=1, concat_axis=0, tiled=True)
    width = owned.shape[2]
    layers = stored_grads.shape[1]
    scale = 1.0 / math.sqrt(width * layers)
    pre = jnp.einsum(
        "rlk,lkj->rlj", owned.astype(jnp.float32), inverse_fisher, precision=lax.Precision.HIGHEST
    )
    mean_square = jnp.mean(pre * pre, axis=2, keepdims=True) + EPS
    normed = (pre * lax.rsqrt(mean_square)).astype(jnp.bfloat16)
    flat = normed.reshape(normed.shape[0], -1)
    order = example_row[0]
    everyone = gather_directly(query_grads, "grp", 0)
    chosen = everyone[query_slot].reshape(everyone.shape[0], -1)
    partial_value = score_block(flat[order], chosen)
    summed = sum_in_two_steps(partial_value, (("lay_0", "lay_1"), "lay_2"), 0)
    return summed * scale


def solution(mesh):
    split = Mesh(
        mesh.devices.reshape(mesh.shape["grp"], 2, 8, 2), ("grp", "lay_0", "lay_1", "lay_2")
    )
    placed = (P(GRP_LAY, None, None), P(LAY, None, None), P("grp", LAY, None), P("grp", None), P())
    return jax.shard_map(
        body, mesh=split, in_specs=placed, out_specs=P(GRP_LAY, None), check_vma=False
    )
```

profile of v0, /device:TPU:1, one launch (start us, length us, event | category | flops | bytes accessed | tf_op | source)
XLA Modules:
  0.0 196.1 jit_solution(13341271138742268284)
XLA Ops:
  0.0 2.6 %broadcast_in_dim.8 = bf16[8,128,1,1024]{3,1,2,0:T(8,128)(2,1)} broadcast(bf16[128,1024]{1,0:T(8,128)(2,1)} %bitcast.40), dimensions={1,3} | broadcast | bytes 2359296 | tf_op jit(solution)/shard_map/broadcast_in_dim | solution.py:17
  2.6 5.9 %all-to-all-start.1 = ((bf16[8,128,1,1024]{3,1,2,0:T(8,128)(2,1)}), bf16[8,128,1,1024]{3,1,2,0:T(8,128)(2,1)S(1)}, u32[]{:S(2)}, u32[]{:S(2)}) async-start(bf16[8,128,1,1024]{3,1,2,0:T(8,128)(2,1)} %broadcast_in_dim.8), calls=%async_computation.1 | async-start | bytes 4194304 | tf_op jit(solution)/shard_map/all_to_all | solution.py:18
  8.5 4.0 %copy.12 = bf16[32,32,1024]{2,0,1:T(8,128)(2,1)} copy(bf16[32,32,1024]{2,1,0:T(8,128)(2,1)} %param.5) | data formatting | bytes 4194304 | tf_op args[0]
  12.5 0.0 copy-start
  12.5 0.0 copy-start.1
  12.5 22.1 %all-to-all-done.1 = bf16[8,128,1,1024]{3,1,2,0:T(8,128)(2,1)S(1)} async-done(((bf16[8,128,1,1024]{3,1,2,0:T(8,128)(2,1)}), bf16[8,128,1,1024]{3,1,2,0:T(8,128)(2,1)S(1)}, u32[]{:S(2)}, u32[]{:S(2)}) %all-to-all-start.1) | async-done | bytes 2097184 | tf_op jit(solution)/shard_map/all_to_all | solution.py:18
  34.6 12.6 %all-to-all-start = ((bf16[32,32,1024]{2,0,1:T(8,128)(2,1)}), bf16[32,32,1024]{2,0,1:T(8,128)(2,1)}, u32[]{:S(2)}, u32[]{:S(2)}) async-start(bf16[32,32,1024]{2,0,1:T(8,128)(2,1)} %copy.12), calls=%async_computation | async-start | bytes 4194304 | tf_op jit(solution)/shard_map/all_to_all | solution.py:56
  47.3 0.0 copy-done
  47.3 0.0 copy-done.1
  47.3 5.4 %gather_fusion.1 = bf16[1024,1024]{1,0:T(8,128)(2,1)} fusion(bf16[1024,1024]{1,0:T(8,128)(2,1)S(1)} %bitcast.38, s32[1024]{0:T(1024)S(1)} %fusion.6), kind=kCustom, calls=%fused_computation.1 | custom fusion | bytes 4198400 | tf_op jit(solution)/shard_map/gather | solution.py:68
  52.7 45.4 %all-to-all-done = bf16[32,32,1024]{2,0,1:T(8,128)(2,1)} async-done(((bf16[32,32,1024]{2,0,1:T(8,128)(2,1)}), bf16[32,32,1024]{2,0,1:T(8,128)(2,1)}, u32[]{:S(2)}, u32[]{:S(2)}) %all-to-all-start) | async-done | bytes 2097184 | tf_op jit(solution)/shard_map/all_to_all | solution.py:56
  98.1 15.7 %fusion = (f32[1024]{0:T(1024)S(1)}, f32[1024,1024]{1,0:T(8,128)S(1)}) fusion(bf16[1024,1024]{1,0:T(8,128)(2,1)} %bitcast.3, f32[1,1024,1024]{2,1,0:T(8,128)} %param.6), kind=kOutput, calls=%fused_computation.4 | convolution fusion | flops 12886998016 | bytes 10489856 | tf_op jit(solution)/shard_map/rlk,lkj->rlj/dot_general | solution.py:60
  113.8 1.9 fusion.4
  115.7 2.9 %copy.13 = bf16[1024,1024]{1,0:T(8,128)(2,1)S(1)} copy(bf16[1024,1024]{0,1:T(8,128)(2,1)} %fusion.4) | data formatting | bytes 4194304 | tf_op jit(solution)/shard_map/reshape | solution.py:65
  118.6 5.4 %gather_fusion = bf16[1024,1024]{1,0:T(8,128)(2,1)} fusion(bf16[1024,1024]{1,0:T(8,128)(2,1)S(1)} %copy.13, s32[1024]{0:T(1024)S(1)} %broadcast_clamp_fusion), kind=kCustom, calls=%fused_computation | custom fusion | bytes 4198400 | tf_op jit(solution)/shard_map/gather | solution.py:69
  124.0 4.6 %convolution_bitcast_fusion = f32[2,16,32,1024]{3,2,0,1:T(8,128)S(1)} fusion(bf16[16,2,32,1024]{3,2,1,0:T(8,128)(2,1)} %bitcast.39, bf16[1024,1024]{1,0:T(8,128)(2,1)} %gather_fusion.1), kind=kOutput, calls=%fused_computation.8 | convolution fusion | flops 2147483648 | bytes 8388608 | tf_op jit(solution)/shard_map/dot_general | solution.py:50
  128.6 0.6 copy.14
  129.2 9.1 %all_to_all.30 = f32[2,16,32,1024]{3,2,1,0:T(8,128)} all-to-all(f32[2,16,32,1024]{3,2,1,0:T(8,128)S(1)} %copy.14), channel_id=1, replica_groups=mesh['grp'=8,'lay_0'=2,'lay_1'=8,'lay_2'=2] {'lay_2'}, dimensions={0} | all-to-all | bytes 8388608 | tf_op jit(solution)/shard_map/all_to_all | solution.py:39
  138.3 2.8 %reduce_sum.28 = f32[16,32,1024]{2,1,0:T(8,128)S(1)} reduce(f32[2,16,32,1024]{3,2,1,0:T(8,128)} %all_to_all.30, f32[]{:T(128)} %constant.1.clone.1), dimensions={0}, to_apply=%region_1.0 | reduce | flops 524288 | bytes 6291460 | tf_op jit(solution)/shard_map/reduce_sum | solution.py:40
  141.1 52.7 %all_to_all.31 = f32[16,32,1024]{2,1,0:T(8,128)} all-to-all(f32[16,32,1024]{2,1,0:T(8,128)S(1)} %reduce_sum.28), channel_id=1, replica_groups=mesh['grp'=8,'lay_0'=2,'lay_1'=8,'lay_2'=2] {'lay_0','lay_1'}, dimensions={0} | all-to-all | bytes 4194304 | tf_op jit(solution)/shard_map/all_to_all | solution.py:46
  193.8 1.7 reduce_sum.29
  195.5 0.7 broadcast_multiply_fusion
  (4 shorter events, 0.0 us)
Async XLA Ops:
  2.6 32.1 %all-to-all-start.1 = ((bf16[8,128,1,1024]{3,1,2,0:T(8,128)(2,1)}), bf16[8,128,1,1024]{3,1,2,0:T(8,128)(2,1)S(1)}, u32[]{:S(2)}, u32[]{:S(2)}) async-start(bf16[8,128,1,1024]{3,1,2,0:T(8,128)(2,1)} %broadcast_in_dim.8), calls=%async_computation.1 | async-start | bytes 4194304 | tf_op jit(solution)/shard_map/all_to_all | solution.py:18
  12.5 34.7 %copy-start = (s32[1,1024]{1,0:T(1,128)S(1)}, s32[1,1024]{1,0:T(1,128)}, u32[]{:S(2)}) copy-start(s32[1,1024]{1,0:T(1,128)} %param.8) | copy-start | bytes 12292
  12.5 34.8 %copy-start.1 = (s32[1024]{0:T(1024)S(1)}, s32[1024]{0:T(1024)}, u32[]{:S(2)}) copy-start(s32[1024]{0:T(1024)} %param.9) | copy-start | bytes 12292
  34.6 63.5 %all-to-all-start = ((bf16[32,32,1024]{2,0,1:T(8,128)(2,1)}), bf16[32,32,1024]{2,0,1:T(8,128)(2,1)}, u32[]{:S(2)}, u32[]{:S(2)}) async-start(bf16[32,32,1024]{2,0,1:T(8,128)(2,1)} %copy.12), calls=%async_computation | async-start | bytes 4194304 | tf_op jit(solution)/shard_map/all_to_all | solution.py:56
where the time goes:
time: 197 us; the launch traced here: 196 us
  waiting for transfers between devices  67.5 us (34%)
  blocking collectives  61.8 us (31%)
  local copies, waits for them, and re-layouts  20.8 us (11%)
  matrix products  20.3 us (10%)
  starting transfers between devices  18.6 us (9%)
  other arithmetic  7.08 us (4%)
    all_to_all x1, blocking collectives, sum_in_two_steps(): return jnp.sum(lax.all_to_all(own, far, 0, 0, tiled=True), axis=0)  52.7 us
    all_to_all x1, waiting for transfers between devices, body(): lax.all_to_all(stored_grads, LAY, split_axis=1, concat_axis=0, tiled=True)  45.4 us
    all_to_all x1, waiting for transfers between devices, sent_to_all(): return lax.all_to_all(copies, axis, split_axis=0, concat_axis=0, tiled=True)  22.1 us
    dot_general x1, matrix products, body(): jnp.einsum('rlk,lkj->rlj', owned.astype(jnp.float32), inverse_fisher, pre...  15.7 us
    all_to_all x1, starting transfers between devices, body(): lax.all_to_all(stored_grads, LAY, split_axis=1, concat_axis=0, tiled=True)  12.6 us
    all_to_all x1, blocking collectives, summed_on_arrival(): lax.all_to_all(pieces, axis, split_axis=0, concat_axis=0, tiled=True)  9.14 us
    all_to_all x1, starting transfers between devices, sent_to_all(): return lax.all_to_all(copies, axis, split_axis=0, concat_axis=0, tiled=True)  5.94 us
    gather x1, local copies, waits for them, and re-layouts, body(): partial_value = score_block(flat[order], chosen)  5.39 us
  transfers between devices with their start and end apart: 2, of which 2 were waited for; matrix products, arithmetic and copies ran while one was open for 5% of the time, Pallas kernels for 0%

commit v1 on v0

v1 whole, which is shorter than its diff:
```python
import math

import jax
import jax.numpy as jnp
from jax import lax
from jax.experimental import pallas as pl
from jax.experimental.pallas import tpu as pltpu
from jax.sharding import Mesh
from jax.sharding import PartitionSpec as P

AXES = ("y", "xl", "xh", "z", "c")
SIZE = {"y": 4, "xl": 2, "xh": 2, "z": 8, "c": 2}
GRP = ("y", "xl")
LAY = ("xh", "z", "c")
EPS = 1e-06
K = 1024
ROWS = 32
BF16 = jnp.bfloat16
F32 = jnp.float32
IN_Z = [(a, b) for a in range(2) for b in range(2)]
FAR_FIRST = (4, 3, 5, 2, 6, 1, 7, 0)


def step_of(g):
    return lax.rem(jnp.where(lax.rem(g, 2) == 1, (g + 1) // 2, 8 - g // 2), 8)


def kernel(
    x_hbm, f_hbm, q_hbm, ex_ref, qs_ref, out_ref,
    x_v, f_v, fh, fl, q_all, qpt, sendbuf, grads, own, other, pick, col, acc,
    xs, xr, zs, zr,
    in_sem, q_send, q_recv, a_send, a_recv, e_send, e_recv, x_send, x_recv, z_send, z_recv,
):
    me = {a: lax.axis_index(a) for a in AXES}
    z, c, xh = me["z"], me["c"], me["xh"]

    def shifted(**off):
        return tuple(lax.rem(me[a] + off.get(a, 0), SIZE[a]) for a in AXES)

    def remote(src, dst, ssem, rsem, dev):
        return pltpu.make_async_remote_copy(
            src_ref=src, dst_ref=dst, send_sem=ssem, recv_sem=rsem,
            device_id=dev, device_id_type=pl.DeviceIdType.MESH,
        )

    load_x = pltpu.make_async_copy(x_hbm, x_v, in_sem.at[0])
    load_f = pltpu.make_async_copy(f_hbm, f_v, in_sem.at[1])
    grp_me = me["y"] * 2 + me["xl"]
    my_q = pl.ds(pl.multiple_of(grp_me * 128, 128), 128)
    load_q = pltpu.make_async_copy(q_hbm, q_all.at[my_q], in_sem.at[2])
    load_x.start()

    barrier = pltpu.get_barrier_semaphore()
    lay_peers = [(a, b, d) for a in range(2) for b in range(8) for d in range(2) if (a, b, d) != (0, 0, 0)]
    grp_peers = [(a, b) for a in range(4) for b in range(2) if (a, b) != (0, 0)]
    for a, b, d in lay_peers:
        pl.semaphore_signal(barrier, inc=1, device_id=shifted(xh=a, z=b, c=d), device_id_type=pl.DeviceIdType.MESH)
    for a, b in grp_peers:
        pl.semaphore_signal(barrier, inc=1, device_id=shifted(y=a, xl=b), device_id_type=pl.DeviceIdType.MESH)
    load_f.start()
    load_q.start()
    load_x.wait()
    pl.semaphore_wait(barrier, len(lay_peers) + len(grp_peers))

    q_out = []
    for i, (a, b) in enumerate(grp_peers):
        copy = remote(q_hbm, q_all.at[my_q], q_send.at[i], q_recv.at[i], shifted(y=a, xl=b))
        copy.start()
        q_out.append(copy)

    row_in = lax.broadcasted_iota(jnp.int32, (128, K), 0)
    col_in = lax.broadcasted_iota(jnp.int32, (128, K), 1)
    source = lax.rem(row_in, 32) * 32 + (row_in // 64) * 16 + lax.rem(row_in // 32, 2)
    base = source - col_in
    slot = pl.multiple_of(xh * 64 + c * 32, 32)

    def a_copy(g, q, sending):
        d = step_of(g)
        a, b = IN_Z[q]
        if sending:
            to = (me["y"], me["xl"], lax.rem(xh + a, 2), lax.rem(z + d, 8), lax.rem(c + b, 2))
            rows = pl.multiple_of(to[2] * 64 + to[4] * 32, 32)
            src, dst = sendbuf.at[g, pl.ds(rows, 32)], grads.at[z, pl.ds(slot, 32)]
        else:
            to = (me["y"], me["xl"], lax.rem(xh + a, 2), lax.rem(z + 8 - d, 8), lax.rem(c + b, 2))
            rows = pl.multiple_of(to[2] * 64 + to[4] * 32, 32)
            src, dst = sendbuf.at[g, pl.ds(rows, 32)], grads.at[to[3], pl.ds(rows, 32)]
        return remote(src, dst, a_send.at[g, q], a_recv.at[g, q], to)

    def prepare(g):
        to_z = lax.rem(z + step_of(g), 8)
        mask = jnp.where(base + 2 * to_z == 0, 1.0, 0.0).astype(BF16)
        sendbuf[g] = jnp.dot(mask, x_v[...], preferred_element_type=F32).astype(BF16)

    prepare(0)
    for q in range(1, 4):
        a_copy(0, q, True).start()
    grads[z, pl.ds(slot, 32)] = sendbuf[0, pl.ds(slot, 32)]

    def prepare_and_send(g, carry):
        prepare(g)
        for q in range(4):
            a_copy(g, q, True).start()
        return carry

    lax.fori_loop(1, 8, prepare_and_send, 0)

    load_f.wait()

    def split(i, carry):
        rows = pl.ds(pl.multiple_of(i * 128, 128), 128)
        f = f_v[rows, :]
        hi = f.astype(BF16)
        fh[rows, :] = hi
        fl[rows, :] = (f - hi.astype(F32)).astype(BF16)
        return carry

    lax.fori_loop(0, 8, split, 0)

    diagonal = lax.broadcasted_iota(jnp.int32, (128, 128), 0) == lax.broadcasted_iota(jnp.int32, (128, 128), 1)

    def as_column(ref, i):
        lanes = pl.ds(pl.multiple_of(i * 128, 128), 128)
        row = jnp.broadcast_to(ref[:, lanes].astype(F32), (128, 128))
        return jnp.sum(jnp.where(diagonal, row, 0.0), axis=1, keepdims=True)

    def columns(i, carry):
        rows = pl.ds(pl.multiple_of(i * 128, 128), 128)
        col[rows, :] = jnp.broadcast_to(as_column(ex_ref, i), (128, 128))
        return carry

    lax.fori_loop(0, 8, columns, 0)

    lane = lax.broadcasted_iota(jnp.int32, (32, 128), 1)
    stored = ((lane // 64) * 512 + lax.rem(lane, 64)).astype(F32)

    def picks(i, carry):
        to_z, to_xh = i // 2, lax.rem(i, 2)
        wanted = col[pl.ds(pl.multiple_of(to_xh * 512 + to_z * 64 + c * 32, 32), 32), :] - stored
        rows = pl.ds(pl.multiple_of(i * 32, 32), 32)
        for zg in range(8):
            pick[zg, rows, :] = jnp.where(wanted == float(zg * 64), 1.0, 0.0).astype(BF16)
        return carry

    lax.fori_loop(0, 16, picks, 0)
    acc[...] = jnp.zeros_like(acc)

    load_q.wait()
    for i, (a, b) in enumerate(grp_peers):
        src = shifted(y=4 - a, xl=2 - b)
        rows = pl.ds(pl.multiple_of((src[0] * 2 + src[1]) * 128, 128), 128)
        remote(q_hbm, q_all.at[rows], q_send.at[i], q_recv.at[i], src).wait_recv()
    lanes_f = lax.broadcasted_iota(jnp.int32, (128, K), 1).astype(F32)

    def ask(i, carry):
        mask = jnp.where(as_column(qs_ref, i) == lanes_f, 1.0, 0.0).astype(BF16)
        chosen = jnp.dot(mask, q_all[...], preferred_element_type=F32)
        lanes = pl.ds(pl.multiple_of(i * 128, 128), 128)
        qpt[:, lanes] = jnp.transpose(chosen).astype(BF16)
        return carry

    lax.fori_loop(0, 8, ask, 0)

    def source_z(g):
        return lax.rem(z + 8 - step_of(g), 8)

    def exchange(g):
        at = source_z(g)
        return remote(own.at[at], other.at[at], e_send.at[g], e_recv.at[g], shifted(c=1))

    def score(g, count):
        for q in range(4 - count, 4):
            a_copy(g, q, False).wait_recv()
        at = source_z(g)
        rows = grads[at]
        pre = jnp.dot(rows, fh[...], preferred_element_type=F32) + jnp.dot(rows, fl[...], preferred_element_type=F32)
        mean_square = jnp.mean(pre * pre, axis=1, keepdims=True) + EPS
        normed = (pre * lax.rsqrt(mean_square)).astype(BF16)
        own[at] = jnp.dot(normed, qpt[...], preferred_element_type=F32)
        exchange(g).start()

    def collect(g):
        exchange(g).wait_recv()
        at = source_z(g)
        both = (own[at] + other[at]).astype(BF16)
        acc[...] += jnp.dot(pick[at], both, preferred_element_type=F32)

    score(0, 3)

    def score_and_collect(g, carry):
        score(g, 4)
        collect(g - 1)
        return carry

    lax.fori_loop(1, 8, score_and_collect, 0)
    collect(7)

    def piece(k, to_xh):
        to_z = lax.rem(z + FAR_FIRST[k], 8)
        return acc[pl.ds(pl.multiple_of(to_z * 64 + to_xh * 32, 32), 32), :]

    def x_copy(k):
        return remote(xs.at[k], xr.at[k], x_send.at[k], x_recv.at[k], shifted(xh=1))

    def z_copy(k):
        return remote(zs.at[k], zr.at[k], z_send.at[k], z_recv.at[k], shifted(z=FAR_FIRST[k]))

    for k in range(8):
        xs[k] = piece(k, 1 - xh).astype(BF16)
        x_copy(k).start()
    for k in range(7):
        x_copy(k).wait_recv()
        zs[k] = (piece(k, xh) + xr[k].astype(F32)).astype(BF16)
        z_copy(k).start()
    x_copy(7).wait_recv()
    total = piece(7, xh) + xr[7].astype(F32)
    for k in range(6, -1, -1):
        z_copy(k).wait_recv()
        total = total + zr[k].astype(F32)
    out_ref[...] = total * (1.0 / math.sqrt(K * 32))

    for copy in q_out:
        copy.wait_send()
    for q in range(1, 4):
        a_copy(0, q, True).wait_send()

    def drain(g, carry):
        for q in range(4):
            a_copy(g, q, True).wait_send()
        exchange(g).wait_send()
        return carry

    lax.fori_loop(1, 8, drain, 0)
    exchange(0).wait_send()
    for k in range(8):
        x_copy(k).wait_send()
        if k < 7:
            z_copy(k).wait_send()


def body(stored_grads, inverse_fisher, query_grads, example_row, query_slot):
    dma = pltpu.SemaphoreType.DMA
    hbm = pl.BlockSpec(memory_space=pl.ANY)
    vmem = pl.BlockSpec(memory_space=pltpu.VMEM)
    return pl.pallas_call(
        kernel,
        out_shape=jax.ShapeDtypeStruct((ROWS, K), F32),
        in_specs=[hbm, hbm, hbm, vmem, vmem],
        out_specs=vmem,
        scratch_shapes=[
            pltpu.VMEM((K, K), BF16),
            pltpu.VMEM((K, K), F32),
            pltpu.VMEM((K, K), BF16),
            pltpu.VMEM((K, K), BF16),
            pltpu.VMEM((K, K), BF16),
            pltpu.VMEM((K, K), BF16),
            pltpu.VMEM((8, 128, K), BF16),
            pltpu.VMEM((8, 128, K), BF16),
            pltpu.VMEM((8, 128, K), F32),
            pltpu.VMEM((8, 128, K), F32),
            pltpu.VMEM((8, 512, 128), BF16),
            pltpu.VMEM((K, 128), F32),
            pltpu.VMEM((512, K), F32),
            pltpu.VMEM((8, ROWS, K), BF16),
            pltpu.VMEM((8, ROWS, K), BF16),
            pltpu.VMEM((8, ROWS, K), BF16),
            pltpu.VMEM((8, ROWS, K), BF16),
            dma((3,)), dma((7,)), dma((7,)), dma((8, 4)), dma((8, 4)), dma((8,)), dma((8,)),
            dma((8,)), dma((8,)), dma((8,)), dma((8,)),
        ],
        name="attribution",
        compiler_params=pltpu.CompilerParams(
            collective_id=0, has_side_effects=True, vmem_limit_bytes=60 * 1024 * 1024
        ),
    )(
        stored_grads.reshape(K, K),
        inverse_fisher.reshape(K, K),
        query_grads.reshape(128, K),
        example_row,
        query_slot.reshape(1, K),
    )


def solution(mesh):
    split = Mesh(mesh.devices.reshape(tuple(SIZE[a] for a in AXES)), AXES)
    placed = (P(AXES, None, None), P(LAY, None, None), P(GRP, LAY, None), P(GRP, None), P())
    return jax.shard_map(body, mesh=split, in_specs=placed, out_specs=P(AXES, None), check_vma=False)
```

time: 197 us -> 94.8 us (0.48)
  Pallas kernels: 0 us -> 93.1 us
  waiting for transfers between devices: 67.5 us -> 0 us
  blocking collectives: 61.8 us -> 0 us
  matrix products: 20.3 us -> 0 us
  local copies, waits for them, and re-layouts: 20.8 us -> 1.57 us
  starting transfers between devices: 18.6 us -> 0 us
  other arithmetic: 7.08 us -> 0 us
    pallas_call x0 -> x1, Pallas kernels: none -> 93.1 us  [body(): pl.pallas_call(kernel, out_shape=jax.ShapeDtypeStruct((ROWS, K), F32), in...]
    all_to_all x2 -> x0, waiting for transfers between devices: 67.5 us -> none  [the longest x1 45.4 us: body(): lax.all_to_all(stored_grads, LAY, split_axis=1, concat_axis=0, tiled=True)]
    all_to_all x2 -> x0, blocking collectives: 61.8 us -> none  [the longest x1 52.7 us: sum_in_two_steps(): return jnp.sum(lax.all_to_all(own, far, 0, 0, tiled=True), axis=0)]
    dot_general x2 -> x0, matrix products: 20.3 us -> none  [the longest x1 15.7 us: body(): jnp.einsum('rlk,lkj->rlj', owned.astype(jnp.float32), inverse_fisher, pre...]
    all_to_all x2 -> x0, starting transfers between devices: 18.6 us -> none  [the longest x1 12.6 us: body(): lax.all_to_all(stored_grads, LAY, split_axis=1, concat_axis=0, tiled=True)]
    gather x2 -> x0, local copies, waits for them, and re-layouts: 10.8 us -> none  [the longest x1 5.39 us: body(): partial_value = score_block(flat[order], chosen)]
    reduce_sum x2 -> x0, other arithmetic: 4.5 us -> none  [the longest x1 2.79 us: summed_on_arrival(): return arrived.sum(axis=0)]
    reshape x1 -> x0, local copies, waits for them, and re-layouts: 2.85 us -> none  [body(): flat = normed.reshape(normed.shape[0], -1)]
  transfers between devices with their start and end apart: 2 -> 0, of which waited for: 2 -> 0; matrix products, arithmetic and copies ran while one was open for 5% -> 0% of each run, Pallas kernels for 0% -> 0%
where the time goes in v1:
time: 94.8 us; the launch traced here: 94.7 us
  Pallas kernels  93.1 us (98%)
  local copies, waits for them, and re-layouts  1.57 us (2%)
    pallas_call x1, Pallas kernels, body(): pl.pallas_call(kernel, out_shape=jax.ShapeDtypeStruct((ROWS, K), F32), in...  93.1 us

profile of v1, /device:TPU:1, one launch (start us, length us, event | category | flops | bytes accessed | tf_op | source)
XLA Modules:
  0.0 94.7 jit_solution(2107953628479740343)
XLA Ops:
  0.0 93.1 %attribution.1 = f32[32,1024]{1,0:T(8,128)} custom-call(bf16[1024,1024]{1,0:T(8,128)(2,1)} %bitcast.5, f32[1024,1024]{1,0:T(8,128)} %bitcast.4, bf16[128,1024]{1,0:T(8,128)(2,1)} %bitcast.6, s32[1,1024]{1,0:T(1,128)} %ex_ref.1, s32[1,1024]{1,0:T(1,128)} %bitcast.7), custom_call_target="tpu_custom_call" | custom-call | tf_op jit(solution)/shard_map/attribution/pallas_call | solution.py:245
  93.1 1.6 %copy.7 = f32[32,1024]{1,0:T(8,128)} copy(f32[32,1024]{1,0:T(8,128)} %attribution.1) | data formatting | bytes 262144

commit v2 on v1

--- a/solution.py
+++ b/solution.py
@@ -18,16 +18,18 @@
 BF16 = jnp.bfloat16
 F32 = jnp.float32
 IN_Z = [(a, b) for a in range(2) for b in range(2)]
+EARLY = 3
+AHEAD = 4
 FAR_FIRST = (4, 3, 5, 2, 6, 1, 7, 0)
 
 
 def step_of(g):
-    return lax.rem(jnp.where(lax.rem(g, 2) == 1, (g + 1) // 2, 8 - g // 2), 8)
+    return jnp.where(lax.rem(g, 2) == 1, (g + 7) // 2, lax.rem((8 - g) // 2, 4))
 
 
 def kernel(
     x_hbm, f_hbm, q_hbm, ex_ref, qs_ref, out_ref,
-    x_v, f_v, fh, fl, q_all, qpt, sendbuf, grads, own, other, pick, col, acc,
+    x_v, f_v, fh, fl, q_all, qpt, sendbuf, grads, normed, own, other, pick, col, acc,
     xs, xr, zs, zr,
     in_sem, q_send, q_recv, a_send, a_recv, e_send, e_recv, x_send, x_recv, z_send, z_recv,
 ):
@@ -52,22 +54,13 @@
 
     barrier = pltpu.get_barrier_semaphore()
     lay_peers = [(a, b, d) for a in range(2) for b in range(8) for d in range(2) if (a, b, d) != (0, 0, 0)]
-    grp_peers = [(a, b) for a in range(4) for b in range(2) if (a, b) != (0, 0)]
+    grp_peers = [(0, 1), (1, 0), (2, 0), (3, 0)]
     for a, b, d in lay_peers:
         pl.semaphore_signal(barrier, inc=1, device_id=shifted(xh=a, z=b, c=d), device_id_type=pl.DeviceIdType.MESH)
     for a, b in grp_peers:
         pl.semaphore_signal(barrier, inc=1, device_id=shifted(y=a, xl=b), device_id_type=pl.DeviceIdType.MESH)
     load_f.start()
     load_q.start()
-    load_x.wait()
-    pl.semaphore_wait(barrier, len(lay_peers) + len(grp_peers))
-
-    q_out = []
-    for i, (a, b) in enumerate(grp_peers):
-        copy = remote(q_hbm, q_all.at[my_q], q_send.at[i], q_recv.at[i], shifted(y=a, xl=b))
-        copy.start()
-        q_out.append(copy)
-
     row_in = lax.broadcasted_iota(jnp.int32, (128, K), 0)
     col_in = lax.broadcasted_iota(jnp.int32, (128, K), 1)
     source = lax.rem(row_in, 32) * 32 + (row_in // 64) * 16 + lax.rem(row_in // 32, 2)
@@ -92,18 +85,47 @@
         mask = jnp.where(base + 2 * to_z == 0, 1.0, 0.0).astype(BF16)
         sendbuf[g] = jnp.dot(mask, x_v[...], preferred_element_type=F32).astype(BF16)
 
-    prepare(0)
+    def prepare_next(g, carry):
+        prepare(g)
+        return carry
+
+    def send(g):
+        for q in range(4):
+            a_copy(g, q, True).start()
+
+    def prepare_and_send(g, carry):
+        prepare(g)
+        send(g)
+        return carry
+
+    load_x.wait()
+    lax.fori_loop(0, 2, prepare_next, 0)
+    pl.semaphore_wait(barrier, len(lay_peers) + len(grp_peers))
+
+    def q_rows(y, xl):
+        return pl.ds(pl.multiple_of((y * 2 + xl) * 128, 128), 128)
+
+    def q_copy(i, sending):
+        a = 0 if i == 0 else (i - 1) % 3 + 1
+        b = 1 if i == 0 else 0
+        if sending:
+            rows = q_rows(me["y"], me["xl"] if i < 4 else 1 - me["xl"])
+            src = q_hbm if i < 4 else q_all.at[rows]
+            to = shifted(y=a, xl=b)
+        else:
+            to = shifted(y=4 - a, xl=b)
+            rows = q_rows(to[0], to[1] if i < 4 else 1 - to[1])
+            src = q_hbm
+        return remote(src, q_all.at[rows], q_send.at[i], q_recv.at[i], to)
+
+    for i in range(4):
+        q_copy(i, True).start()
+    send(1)
     for q in range(1, 4):
         a_copy(0, q, True).start()
+    lax.fori_loop(2, AHEAD + 1, prepare_and_send, 0)
+    lax.fori_loop(AHEAD + 1, 8, prepare_next, 0)
     grads[z, pl.ds(slot, 32)] = sendbuf[0, pl.ds(slot, 32)]
-
-    def prepare_and_send(g, carry):
-        prepare(g)
-        for q in range(4):
-            a_copy(g, q, True).start()
-        return carry
-
-    lax.fori_loop(1, 8, prepare_and_send, 0)
 
     load_f.wait()
 
@@ -117,6 +139,10 @@
 
     lax.fori_loop(0, 8, split, 0)
 
+    q_copy(0, False).wait_recv()
+    for i in range(4, 7):
+        q_copy(i, True).start()
+
     diagonal = lax.broadcasted_iota(jnp.int32, (128, 128), 0) == lax.broadcasted_iota(jnp.int32, (128, 128), 1)
 
     def as_column(ref, i):
@@ -145,11 +171,40 @@
     lax.fori_loop(0, 16, picks, 0)
     acc[...] = jnp.zeros_like(acc)
 
+    def source_z(g):
+        return lax.rem(z + 8 - step_of(g), 8)
+
+    def arrived(g):
+        for q in range(4):
+            a_copy(g, q, True).wait_send()
+
+        @pl.when(g + AHEAD < 8)
+        def _():
+            send(g + AHEAD)
+
+        for q in range(4):
+            a_copy(g, q, False).wait_recv()
+
+    def normalise(g):
+        at = source_z(g)
+        rows = grads[at]
+        pre = jnp.dot(rows, fh[...], preferred_element_type=F32) + jnp.dot(rows, fl[...], preferred_element_type=F32)
+        mean_square = jnp.mean(pre * pre, axis=1, keepdims=True) + EPS
+        normed[at] = (pre * lax.rsqrt(mean_square)).astype(BF16)
+
+    def normalise_next(g, carry):
+        arrived(g)
+        normalise(g)
+        return carry
+
+    for q in range(1, 4):
+        a_copy(0, q, False).wait_recv()
+    normalise(0)
+    lax.fori_loop(1, EARLY, normalise_next, 0)
+
     load_q.wait()
-    for i, (a, b) in enumerate(grp_peers):
-        src = shifted(y=4 - a, xl=2 - b)
-        rows = pl.ds(pl.multiple_of((src[0] * 2 + src[1]) * 128, 128), 128)
-        remote(q_hbm, q_all.at[rows], q_send.at[i], q_recv.at[i], src).wait_recv()
+    for i in range(1, 7):
+        q_copy(i, False).wait_recv()
     lanes_f = lax.broadcasted_iota(jnp.int32, (128, K), 1).astype(F32)
 
     def ask(i, carry):
@@ -161,22 +216,13 @@
 
     lax.fori_loop(0, 8, ask, 0)
 
-    def source_z(g):
-        return lax.rem(z + 8 - step_of(g), 8)
-
     def exchange(g):
         at = source_z(g)
         return remote(own.at[at], other.at[at], e_send.at[g], e_recv.at[g], shifted(c=1))
 
-    def score(g, count):
-        for q in range(4 - count, 4):
-            a_copy(g, q, False).wait_recv()
+    def score(g):
         at = source_z(g)
-        rows = grads[at]
-        pre = jnp.dot(rows, fh[...], preferred_element_type=F32) + jnp.dot(rows, fl[...], preferred_element_type=F32)
-        mean_square = jnp.mean(pre * pre, axis=1, keepdims=True) + EPS
-        normed = (pre * lax.rsqrt(mean_square)).astype(BF16)
-        own[at] = jnp.dot(normed, qpt[...], preferred_element_type=F32)
+        own[at] = jnp.dot(normed[at], qpt[...], preferred_element_type=F32)
         exchange(g).start()
 
     def collect(g):
@@ -185,14 +231,23 @@
         both = (own[at] + other[at]).astype(BF16)
         acc[...] += jnp.dot(pick[at], both, preferred_element_type=F32)
 
-    score(0, 3)
-
-    def score_and_collect(g, carry):
-        score(g, 4)
+    score(0)
+
+    def score_early(g, carry):
+        score(g)
         collect(g - 1)
         return carry
 
-    lax.fori_loop(1, 8, score_and_collect, 0)
+    lax.fori_loop(1, EARLY, score_early, 0)
+
+    def score_late(g, carry):
+        arrived(g)
+        normalise(g)
+        score(g)
+        collect(g - 1)
+        return carry
+
+    lax.fori_loop(EARLY, 8, score_late, 0)
     collect(7)
 
     def piece(k, to_xh):
@@ -219,14 +274,12 @@
         total = total + zr[k].astype(F32)
     out_ref[...] = total * (1.0 / math.sqrt(K * 32))
 
-    for copy in q_out:
-        copy.wait_send()
+    for i in range(7):
+        q_copy(i, True).wait_send()
     for q in range(1, 4):
         a_copy(0, q, True).wait_send()
 
     def drain(g, carry):
-        for q in range(4):
-            a_copy(g, q, True).wait_send()
         exchange(g).wait_send()
         return carry
 
@@ -254,6 +307,7 @@
             pltpu.VMEM((K, K), BF16),
             pltpu.VMEM((K, K), BF16),
             pltpu.VMEM((K, K), BF16),
+            pltpu.VMEM((8, 128, K), BF16),
             pltpu.VMEM((8, 128, K), BF16),
             pltpu.VMEM((8, 128, K), BF16),
             pltpu.VMEM((8, 128, K), F32),

time: 94.8 us -> 86.9 us (0.917)
  Pallas kernels: 93.1 us -> 85.2 us
    pallas_call x1, Pallas kernels: 93.1 us -> 85.2 us  [body(): pl.pallas_call(kernel, out_shape=jax.ShapeDtypeStruct((ROWS, K), F32), in...]
where the time goes in v2:
time: 86.9 us; the launch traced here: 86.8 us
  Pallas kernels  85.2 us (98%)
  local copies, waits for them, and re-layouts  1.57 us (2%)
    pallas_call x1, Pallas kernels, body(): pl.pallas_call(kernel, out_shape=jax.ShapeDtypeStruct((ROWS, K), F32), in...  85.2 us

profile of v2, /device:TPU:1, one launch (start us, length us, event | category | flops | bytes accessed | tf_op | source)
XLA Modules:
  0.0 86.8 jit_solution(5094032068194020580)
XLA Ops:
  0.0 85.2 %attribution.1 = f32[32,1024]{1,0:T(8,128)} custom-call(bf16[1024,1024]{1,0:T(8,128)(2,1)} %bitcast.5, f32[1024,1024]{1,0:T(8,128)} %bitcast.4, bf16[128,1024]{1,0:T(8,128)(2,1)} %bitcast.6, s32[1,1024]{1,0:T(1,128)} %ex_ref.1, s32[1,1024]{1,0:T(1,128)} %bitcast.7), custom_call_target="tpu_custom_call" | custom-call | tf_op jit(solution)/shard_map/attribution/pallas_call | solution.py:298
  85.2 1.6 %copy.7 = f32[32,1024]{1,0:T(8,128)} copy(f32[32,1024]{1,0:T(8,128)} %attribution.1) | data formatting | bytes 262144

commit v3 on v2

--- a/solution.py
+++ b/solution.py
@@ -28,7 +28,7 @@
 
 
 def kernel(
-    x_hbm, f_hbm, q_hbm, ex_ref, qs_ref, out_ref,
+    x_hbm, f_hbm, q_hbm, order_ref, out_ref,
     x_v, f_v, fh, fl, q_all, qpt, sendbuf, grads, normed, own, other, pick, col, acc,
     xs, xr, zs, zr,
     in_sem, q_send, q_recv, a_send, a_recv, e_send, e_recv, x_send, x_recv, z_send, z_recv,
@@ -55,6 +55,7 @@
     barrier = pltpu.get_barrier_semaphore()
     lay_peers = [(a, b, d) for a in range(2) for b in range(8) for d in range(2) if (a, b, d) != (0, 0, 0)]
     grp_peers = [(0, 1), (1, 0), (2, 0), (3, 0)]
+    lay_peers.sort(key=lambda p: -(2 * p[0] + min(p[1], 8 - p[1])))
     for a, b, d in lay_peers:
         pl.semaphore_signal(barrier, inc=1, device_id=shifted(xh=a, z=b, c=d), device_id_type=pl.DeviceIdType.MESH)
     for a, b in grp_peers:
@@ -90,7 +91,7 @@
         return carry
 
     def send(g):
-        for q in range(4):
+        for q in (2, 3, 0, 1):
             a_copy(g, q, True).start()
 
     def prepare_and_send(g, carry):
@@ -145,14 +146,14 @@
 
     diagonal = lax.broadcasted_iota(jnp.int32, (128, 128), 0) == lax.broadcasted_iota(jnp.int32, (128, 128), 1)
 
-    def as_column(ref, i):
+    def as_column(which, i):
         lanes = pl.ds(pl.multiple_of(i * 128, 128), 128)
-        row = jnp.broadcast_to(ref[:, lanes].astype(F32), (128, 128))
+        row = jnp.broadcast_to(order_ref[pl.ds(which, 1), lanes].astype(F32), (128, 128))
         return jnp.sum(jnp.where(diagonal, row, 0.0), axis=1, keepdims=True)
 
     def columns(i, carry):
         rows = pl.ds(pl.multiple_of(i * 128, 128), 128)
-        col[rows, :] = jnp.broadcast_to(as_column(ex_ref, i), (128, 128))
+        col[rows, :] = jnp.broadcast_to(as_column(0, i), (128, 128))
         return carry
 
     lax.fori_loop(0, 8, columns, 0)
@@ -208,7 +209,7 @@
     lanes_f = lax.broadcasted_iota(jnp.int32, (128, K), 1).astype(F32)
 
     def ask(i, carry):
-        mask = jnp.where(as_column(qs_ref, i) == lanes_f, 1.0, 0.0).astype(BF16)
+        mask = jnp.where(as_column(1, i) == lanes_f, 1.0, 0.0).astype(BF16)
         chosen = jnp.dot(mask, q_all[...], preferred_element_type=F32)
         lanes = pl.ds(pl.multiple_of(i * 128, 128), 128)
         qpt[:, lanes] = jnp.transpose(chosen).astype(BF16)
@@ -272,7 +273,7 @@
     for k in range(6, -1, -1):
         z_copy(k).wait_recv()
         total = total + zr[k].astype(F32)
-    out_ref[...] = total * (1.0 / math.sqrt(K * 32))
+    out_ref[...] = total
 
     for i in range(7):
         q_copy(i, True).wait_send()
@@ -293,12 +294,12 @@
 
 def body(stored_grads, inverse_fisher, query_grads, example_row, query_slot):
     dma = pltpu.SemaphoreType.DMA
-    hbm = pl.BlockSpec(memory_space=pl.ANY)
+    hbm = pl.BlockSpec(memory_space=pltpu.HBM)
     vmem = pl.BlockSpec(memory_space=pltpu.VMEM)
-    return pl.pallas_call(
+    total = pl.pallas_call(
         kernel,
         out_shape=jax.ShapeDtypeStruct((ROWS, K), F32),
-        in_specs=[hbm, hbm, hbm, vmem, vmem],
+        in_specs=[hbm, hbm, hbm, vmem],
         out_specs=vmem,
         scratch_shapes=[
             pltpu.VMEM((K, K), BF16),
@@ -324,15 +325,15 @@
         ],
         name="attribution",
         compiler_params=pltpu.CompilerParams(
-            collective_id=0, has_side_effects=True, vmem_limit_bytes=60 * 1024 * 1024
+            collective_id=0, has_side_effects=True, vmem_limit_bytes=55000 * 1024
         ),
     )(
         stored_grads.reshape(K, K),
         inverse_fisher.reshape(K, K),
         query_grads.reshape(128, K),
-        example_row,
-        query_slot.reshape(1, K),
+        jnp.concatenate([example_row, query_slot.reshape(1, K)], axis=0),
     )
+    return total * (1.0 / math.sqrt(K * 32))
 
 
 def solution(mesh):

time: 86.9 us -> 84.2 us (0.969)
  Pallas kernels: 85.2 us -> 82.7 us
  local copies, waits for them, and re-layouts: 1.57 us -> 0 us
  other arithmetic: 0 us -> 1.38 us
    pallas_call x1, Pallas kernels: 85.2 us -> 82.7 us  [body(): pl.pallas_call(kernel, out_shape=jax.ShapeDtypeStruct((ROWS, K), F32), in...]
    unnamed x1 -> x0, local copies, waits for them, and re-layouts: 1.57 us -> none
where the time goes in v3:
time: 84.2 us; the launch traced here: 84.1 us
  Pallas kernels  82.7 us (98%)
  other arithmetic  1.38 us (2%)
    pallas_call x1, Pallas kernels, body(): pl.pallas_call(kernel, out_shape=jax.ShapeDtypeStruct((ROWS, K), F32), in...  82.7 us

profile of v3, /device:TPU:1, one launch (start us, length us, event | category | flops | bytes accessed | tf_op | source)
XLA Modules:
  0.0 84.1 jit_solution(9538034361817772875)
XLA Ops:
  0.0 0.7 pad_add_fusion.order_ref
  0.7 82.7 %attribution.1 = f32[32,1024]{1,0:T(8,128)S(1)} custom-call(bf16[1024,1024]{1,0:T(8,128)(2,1)} %bitcast.5, f32[1024,1024]{1,0:T(8,128)} %bitcast.4, bf16[128,1024]{1,0:T(8,128)(2,1)} %bitcast.6, s32[2,1024]{1,0:T(2,128)S(1)} %pad_add_fusion.order_ref), custom_call_target="tpu_custom_call" | custom-call | tf_op jit(solution)/shard_map/attribution/pallas_call | solution.py:299
  83.4 0.7 broadcast_multiply_fusion

commit v4 on v3

--- a/solution.py
+++ b/solution.py
@@ -18,13 +18,16 @@
 BF16 = jnp.bfloat16
 F32 = jnp.float32
 IN_Z = [(a, b) for a in range(2) for b in range(2)]
-EARLY = 3
-AHEAD = 4
+EARLY = 2
+AHEAD = 5
 FAR_FIRST = (4, 3, 5, 2, 6, 1, 7, 0)
 
 
 def step_of(g):
-    return jnp.where(lax.rem(g, 2) == 1, (g + 7) // 2, lax.rem((8 - g) // 2, 4))
+    step = 0
+    for i, d in enumerate((0, 3, 5, 4, 2, 6, 1, 7)):
+        step = jnp.where(g == i, d, step)
+    return step
 
 
 def kernel(
@@ -236,7 +239,6 @@
 
     def score_early(g, carry):
         score(g)
-        collect(g - 1)
         return carry
 
     lax.fori_loop(1, EARLY, score_early, 0)
@@ -245,10 +247,11 @@
         arrived(g)
         normalise(g)
         score(g)
-        collect(g - 1)
+        collect(g - 2)
         return carry
 
     lax.fori_loop(EARLY, 8, score_late, 0)
+    collect(6)
     collect(7)
 
     def piece(k, to_xh):

time: 84.2 us -> 83.2 us (0.988)
  Pallas kernels: 82.7 us -> 81.7 us
    pallas_call x1, Pallas kernels: 82.7 us -> 81.7 us  [body(): pl.pallas_call(kernel, out_shape=jax.ShapeDtypeStruct((ROWS, K), F32), in...]
where the time goes in v4:
time: 83.2 us; the launch traced here: 83.1 us
  Pallas kernels  81.7 us (98%)
  other arithmetic  1.38 us (2%)
    pallas_call x1, Pallas kernels, body(): pl.pallas_call(kernel, out_shape=jax.ShapeDtypeStruct((ROWS, K), F32), in...  81.7 us

profile of v4, /device:TPU:1, one launch (start us, length us, event | category | flops | bytes accessed | tf_op | source)
XLA Modules:
  0.0 83.1 jit_solution(4441362538552688385)
XLA Ops:
  0.0 0.7 pad_add_fusion.order_ref
  0.7 81.7 %attribution.1 = f32[32,1024]{1,0:T(8,128)S(1)} custom-call(bf16[1024,1024]{1,0:T(8,128)(2,1)} %bitcast.5, f32[1024,1024]{1,0:T(8,128)} %bitcast.4, bf16[128,1024]{1,0:T(8,128)(2,1)} %bitcast.6, s32[2,1024]{1,0:T(2,128)S(1)} %pad_add_fusion.order_ref), custom_call_target="tpu_custom_call" | custom-call | tf_op jit(solution)/shard_map/attribution/pallas_call | solution.py:302
  82.4 0.7 broadcast_multiply_fusion

commit v5 on v4

--- a/solution.py
+++ b/solution.py
@@ -239,6 +239,7 @@
 
     def score_early(g, carry):
         score(g)
+        collect(g - 1)
         return carry
 
     lax.fori_loop(1, EARLY, score_early, 0)
@@ -247,11 +248,10 @@
         arrived(g)
         normalise(g)
         score(g)
-        collect(g - 2)
+        collect(g - 1)
         return carry
 
     lax.fori_loop(EARLY, 8, score_late, 0)
-    collect(6)
     collect(7)
 
     def piece(k, to_xh):

time: 83.2 us -> 82.9 us (level)
  no operation moved by 1% of the time
where the time goes in v5:
time: 82.9 us; the launch traced here: 82.8 us
  Pallas kernels  81.4 us (98%)
  other arithmetic  1.38 us (2%)
    pallas_call x1, Pallas kernels, body(): pl.pallas_call(kernel, out_shape=jax.ShapeDtypeStruct((ROWS, K), F32), in...  81.4 us

profile of v5, /device:TPU:1, one launch (start us, length us, event | category | flops | bytes accessed | tf_op | source)
XLA Modules:
  0.0 82.8 jit_solution(18862536943840568)
XLA Ops:
  0.0 0.7 pad_add_fusion.order_ref
  0.7 81.4 %attribution.1 = f32[32,1024]{1,0:T(8,128)S(1)} custom-call(bf16[1024,1024]{1,0:T(8,128)(2,1)} %bitcast.5, f32[1024,1024]{1,0:T(8,128)} %bitcast.4, bf16[128,1024]{1,0:T(8,128)(2,1)} %bitcast.6, s32[2,1024]{1,0:T(2,128)S(1)} %pad_add_fusion.order_ref), custom_call_target="tpu_custom_call" | custom-call | tf_op jit(solution)/shard_map/attribution/pallas_call | solution.py:302
  82.1 0.7 broadcast_multiply_fusion
